TPU v7x, 256 devices: a whole 4x4x8 slice. The times are simulated.
256 devices in a mesh: group: 8 (over x, core), dom: 32 (over y, z).
Axes of the slice: x: 4, y: 4, z: 8, core: 2. Of those that a mesh axis runs over, the one named last changes fastest.
Arguments:
- flow_state: float32 [5, 1048576], P(None, ('group', 'dom')), may hold values from -6 to 6
- right_side: float32 [5, 1048576], P(None, ('group', 'dom')), may hold values from -6 to 6
- coupling: float32 [1048576], P(('group', 'dom')), may hold values from 0.03 to 0.3
- pivot_inv: float32 [32, 25, 32768], P(None, None, ('group', 'dom'))
- lower_blocks: float32 [32, 25, 32768], P(None, None, ('group', 'dom'))
- upper_blocks: float32 [32, 25, 32768], P(None, None, ('group', 'dom')), may hold values from -0.15 to 0.15
- face_up: int32 [8, 32, 256], P('group', 'dom'), may hold values from 0 to 4095, as said below
- face_down: int32 [8, 32, 256], P('group', 'dom'), may hold values from 0 to 4095, as said below
- coef_up: float32 [8, 32, 256], P('group', 'dom'), may hold values from 0.1 to 0.5
- coef_down: float32 [8, 32, 256], P('group', 'dom'), may hold values from 0.1 to 0.5
- send_cell: int32 [32, 32768], P(None, ('group', 'dom')), may hold values from 0 to 4095, as said below
- line_src: int32 [32, 32768], P(None, ('group', 'dom')), may hold values from 0 to 8191, as said below
- ret_slot: int32 [32, 32768], P(None, ('group', 'dom')), may hold values from 0 to 4095, as said below
- cell_src: int32 [1048576], P(('group', 'dom')), may hold values from 0 to 8191, as said below
Outputs:
- solution: float32 [5, 1048576], P(None, ('group', 'dom'))
- drive_next: float32 [5, 1048576], P(None, ('group', 'dom'))
Inputs may be any that keep to these rules, and one draw needn't show every extreme that they name: Within a group, the cells named by send_cell for all owners together with the own cells named by line_src cover every cell exactly once; for each sender and owner, the first entries, as many as the cells that sender sends that owner (at most 128), are used and the rest are unused; at most 128 cells go from one partition to one other owner, and this is reached for many pairs in every draw; a partition sends none of its cells to itself through send_cell. `ret_slot`: used entries point at the slot that holds the sent cell. `cell_src`: each cell's value returns to it from the slot that took it. `face_up`: distinct cells within one partition's list. `face_down`: distinct cells within one partition's list.
All inputs are finite; a program needn't handle non-finite values.
Results may differ from a plain program's by a relative error of at most 0.0001.
Values sent between devices are 32-bit elements; how exact they have to be, the bound alone decides.
A program may use at most 192 MiB of HBM per device.

v0:
```python
import jax
import jax.numpy as jnp
from jax import lax
from jax.sharding import PartitionSpec as P

SWEEPS = 2


def shifted(block, axis, distance):
    devices = range(lax.axis_size(axis))
    route = [(i - distance, i) for i in devices if i - distance in devices]
    return lax.ppermute(block, axis, route)


def apply_block(matrix, vector):
    nvar = vector.shape[0]
    return jnp.sum(matrix.reshape(nvar, nvar, -1) * vector[None, :, :], axis=1)


def solve_lines(line_vals, pivot_inv, lower_blocks, upper_blocks):
    nvar = line_vals.shape[0]
    line_len, _, line_count = pivot_inv.shape
    blocks = line_vals.reshape(nvar, line_len, line_count)
    forward_vals = []
    previous = None
    for cell_position in range(line_len):
        reduced = blocks[:, cell_position]
        if cell_position > 0:
            reduced = reduced - apply_block(lower_blocks[cell_position], previous)
        previous = apply_block(pivot_inv[cell_position], reduced)
        forward_vals.append(previous)
    results = [None] * line_len
    later = forward_vals[-1]
    results[-1] = later
    for cell_position in range(line_len - 2, -1, -1):
        later = forward_vals[cell_position] - apply_block(upper_blocks[cell_position], later)
        results[cell_position] = later
    return jnp.stack(results, axis=1).reshape(nvar, line_len * line_count)


def shards(
    flow_state,
    right_side,
    coupling,
    pivot_inv,
    lower_blocks,
    upper_blocks,
    face_up,
    face_down,
    coef_up,
    coef_down,
    send_cell,
    line_src,
    ret_slot,
    cell_src,
):
    nvar = flow_state.shape[0]
    cell_count = flow_state.shape[1]
    domains = lax.axis_size("dom")
    capacity = send_cell.shape[1]
    pool_base = domains * capacity
    up_cells = face_up.reshape(-1)
    down_cells = face_down.reshape(-1)
    up_coef = coef_up.reshape(-1)
    down_coef = coef_down.reshape(-1)
    slot_map = line_src.reshape(-1)

    def drive_term(values):
        zeros_col = jnp.zeros((nvar, 1), jnp.float32)
        beside = jnp.concatenate([zeros_col, values[:, :-1]], 1) + jnp.concatenate(
            [values[:, 1:], zeros_col], 1
        )
        total = right_side + coupling[None, :] * beside
        up_vals = values[:, up_cells]
        down_vals = values[:, down_cells]
        from_below = shifted(up_vals, "group", 1)
        from_above = shifted(down_vals, "group", -1)
        total = total.at[:, down_cells].add(down_coef[None, :] * from_below)
        total = total.at[:, up_cells].add(up_coef[None, :] * from_above)
        return total

    peer_maps = lax.all_to_all(send_cell, "dom", split_axis=0, concat_axis=0, tiled=True)
    remote = slot_map < pool_base
    clipped = jnp.minimum(slot_map, pool_base - 1)
    global_idx = clipped // capacity * cell_count + peer_maps.reshape(-1)[clipped]
    own_idx = jnp.clip(slot_map - pool_base, 0, cell_count - 1)
    state_now = flow_state
    for sweep_idx in range(SWEEPS):
        drive_vals = drive_term(state_now)
        whole = lax.all_gather(drive_vals, "dom", axis=1, tiled=True)
        line_vals = jnp.where(remote[None, :], whole[:, global_idx], drive_vals[:, own_idx])
        solved = solve_lines(line_vals, pivot_inv, lower_blocks, upper_blocks)
        outgoing = solved[:, ret_slot]
        returned = lax.all_to_all(outgoing, "dom", split_axis=1, concat_axis=1, tiled=True)
        pooled = jnp.concatenate([returned.reshape(nvar, pool_base), solved], 1)
        state_now = pooled[:, cell_src]
    drive_last = drive_term(state_now)
    return (state_now, drive_last)


def solution(mesh):
    return jax.shard_map(
        shards,
        mesh=mesh,
        in_specs=(
            P(None, ("group", "dom")),
            P(None, ("group", "dom")),
            P(("group", "dom")),
            P(None, None, ("group", "dom")),
            P(None, None, ("group", "dom")),
            P(None, None, ("group", "dom")),
            P("group", "dom", None),
            P("group", "dom", None),
            P("group", "dom", None),
            P("group", "dom", None),
            P(None, ("group", "dom")),
            P(None, ("group", "dom")),
            P(None, ("group", "dom")),
            P(("group", "dom")),
        ),
        out_specs=(P(None, ("group", "dom")), P(None, ("group", "dom"))),
        check_vma=False,
    )
```

profile of v0, /device:TPU:1, one launch (start us, length us, event | category | flops | bytes accessed | tf_op | source)
XLA Modules:
  0.0 1229.1 jit_solution(4603384156076529335)
XLA Ops:
  8.7 1.5 copy.514
  11.0 4.5 collective-permute-start
  16.2 1.9 collective-permute-start.1
  19.1 2.8 scatter_custom_fusion
  22.5 2.8 scatter_custom_fusion.1
  26.7 11.2 all-to-all-start
  40.2 3.4 slice_reduce_fusion.2
  47.5 1.3 fusion.25
  48.9 2.0 slice_reduce_fusion.5
  50.9 1.3 reshape_squeeze.376
  52.2 1.3 reshape_squeeze.379
  53.5 1.3 reshape_squeeze.378
  54.8 1.3 reshape_squeeze.382
  56.2 1.3 reshape_squeeze.381
  57.5 1.3 reshape_squeeze.385
  58.8 1.3 reshape_squeeze.384
  60.1 1.3 reshape_squeeze.388
  61.4 1.3 reshape_squeeze.387
  63.4 1.3 reshape_squeeze.390
  65.3 1.3 reshape_squeeze.393
  67.2 1.3 reshape_squeeze.396
  69.2 1.3 reshape_squeeze.399
  74.1 1.3 reshape_squeeze.412
  75.4 1.3 reshape_squeeze.411
  76.7 1.3 reshape_squeeze.415
  78.0 1.3 reshape_squeeze.414
  79.4 1.3 reshape_squeeze.418
  80.7 1.3 reshape_squeeze.417
  83.3 1.3 reshape_squeeze.420
  84.6 1.3 reshape_squeeze.424
  85.9 1.3 reshape_squeeze.423
  87.9 1.3 reshape_squeeze.426
  89.8 1.3 reshape_squeeze.429
  95.0 14.1 %gather_fusion.4 = f32[4096,5]{1,0:T(8,128)} fusion(f32[5,4096]{0,1:T(8,128)S(1)} %copy-done.1, s32[4096]{0:T(1024)S(1)} %broadcast_clamp_fusion.1), kind=kCustom, calls=%fused_computation.4 | custom fusion | bytes 180224 | tf_op jit(solution)/shard_map/gather | solution.py:91
  109.0 2.2 copy.518
  111.2 23.2 %gather_fusion.2 = s32[4096]{0:T(1024)S(1)} fusion(s32[4096]{0:T(1024)S(1)} %bitcast.448, s32[4096]{0:T(1024)} %broadcast_clamp_fusion.2), kind=kCustom, calls=%fused_computation.2 | custom fusion | bytes 49152 | tf_op jit(solution)/shard_map/gather | solution.py:85
  134.5 325.0 %all-gather.3.cloned.1.call-done = f32[5,131072]{0,1:T(8,128)} async-done(((f32[5,4096]{0,1:T(8,128)}), f32[5,131072]{0,1:T(8,128)}) %all-gather.3.cloned.1.call-update) | async-done | bytes 2621456 | tf_op jit(solution)/shard_map/all_gather | solution.py:90
  459.5 63.9 %gather_fusion.3 = f32[4096,5]{1,0:T(8,128)S(1)} fusion(f32[5,131072]{0,1:T(8,128)} %all-gather.3.cloned.1.call-done, s32[4096]{0:T(1024)S(1)} %broadcast_clamp_fusion), kind=kCustom, calls=%fused_computation.3 | custom fusion | bytes 180224 | tf_op jit(solution)/shard_map/gather | solution.py:91
  559.0 14.1 %gather_fusion.5 = f32[4096,5]{1,0:T(8,128)} fusion(f32[5,4096]{0,1:T(8,128)S(1)} %bitcast.451, s32[4096]{0:T(1024)S(1)} %copy-done.17), kind=kCustom, calls=%fused_computation.5 | custom fusion | bytes 180224 | tf_op jit(solution)/shard_map/gather | solution.py:93
  573.1 2.2 copy.520
  575.3 14.3 %all_to_all.19 = f32[5,32,128]{2,0,1:T(8,128)S(1)} all-to-all(f32[5,32,128]{2,0,1:T(8,128)S(1)} %bitcast.468), channel_id=1, replica_groups=mesh['group'=8,'dom'=32] {'dom'}, dimensions={1} | all-to-all | bytes 163840 | tf_op jit(solution)/shard_map/all_to_all | solution.py:94
  589.6 2.0 copy.521
  591.5 3.8 pad_maximum_fusion
  595.3 13.0 %gather_fusion.6 = f32[4096,5]{1,0:T(8,128)S(1)} fusion(f32[5,8192]{0,1:T(8,128)} %pad_maximum_fusion, s32[4096]{0:T(1024)S(1)} %copy-done.12), kind=kCustom, calls=%fused_computation.6 | custom fusion | bytes 180224 | tf_op jit(solution)/shard_map/gather | solution.py:96
  608.9 1.6 gather_fusion.7
  610.6 1.5 gather_fusion.8
  612.1 5.8 collective-permute-start.2
  617.9 2.1 collective-permute-start.3
  620.8 3.2 scatter_custom_fusion.2
  624.5 3.1 scatter_custom_fusion.3
  627.7 1.3 copy-done.2
  629.0 12.4 %gather_fusion.10 = f32[4096,5]{1,0:T(8,128)S(1)} fusion(f32[5,4096]{0,1:T(8,128)} %copy-done.2, s32[4096]{0:T(1024)S(1)} %copy-done.9), kind=kCustom, calls=%fused_computation.10 | custom fusion | bytes 180224 | tf_op jit(solution)/shard_map/gather | solution.py:91
  642.0 412.6 %all-gather.5.cloned.1.call-done = f32[5,131072]{0,1:T(8,128)} async-done(((f32[5,4096]{0,1:T(8,128)}), f32[5,131072]{0,1:T(8,128)}) %all-gather.5.cloned.1.call-update) | async-done | bytes 2621456 | tf_op jit(solution)/shard_map/all_gather | solution.py:90
  1054.6 63.9 %gather_fusion.9 = f32[4096,5]{1,0:T(8,128)S(1)} fusion(f32[5,131072]{0,1:T(8,128)} %all-gather.5.cloned.1.call-done, s32[4096]{0:T(1024)S(1)} %copy-done.11), kind=kCustom, calls=%fused_computation.9 | custom fusion | bytes 180224 | tf_op jit(solution)/shard_map/gather | solution.py:91
  1154.0 14.1 %gather_fusion.11 = f32[4096,5]{1,0:T(8,128)} fusion(f32[5,4096]{0,1:T(8,128)S(1)} %bitcast.449, s32[4096]{0:T(1024)S(1)} %copy-done.18), kind=kCustom, calls=%fused_computation.11 | custom fusion | bytes 180224 | tf_op jit(solution)/shard_map/gather | solution.py:93
  1168.1 2.2 copy.529
  1170.3 14.3 %all_to_all.20 = f32[5,32,128]{2,0,1:T(8,128)S(1)} all-to-all(f32[5,32,128]{2,0,1:T(8,128)S(1)} %bitcast.469), channel_id=1, replica_groups=mesh['group'=8,'dom'=32] {'dom'}, dimensions={1} | all-to-all | bytes 163840 | tf_op jit(solution)/shard_map/all_to_all | solution.py:94
  1184.6 2.0 copy.530
  1186.6 3.8 pad_maximum_fusion.1
  1190.4 13.0 %gather_fusion.12 = f32[4096,5]{1,0:T(8,128)S(1)} fusion(f32[5,8192]{0,1:T(8,128)} %pad_maximum_fusion.1, s32[4096]{0:T(1024)S(1)} %copy-done.13), kind=kCustom, calls=%fused_computation.12 | custom fusion | bytes 180224 | tf_op jit(solution)/shard_map/gather | solution.py:96
  1206.0 5.8 collective-permute-start.4
  1211.7 1.9 collective-permute-start.5
  1214.5 2.9 scatter_custom_fusion.4
  1218.0 2.9 scatter_custom_fusion.5
  (598 shorter events, 100.2 us)
Async XLA Ops:
  7.2 11.0 copy-start.3
  7.2 11.1 copy-start.5
  7.2 11.1 copy-start.14
  7.2 452.3 %all-gather.3.cloned.1.call-start = ((), (), s32[]{:S(2)}) async-start(), calls=%async_computation.3 | async-start | bytes 69206016 | tf_op jit(solution)/shard_map/all_gather | solution.py:90
  8.0 11.1 copy-start.51
  8.7 13.8 %copy-start.50 = (s32[256,1]{0,1:T(1,128)}, s32[256,1]{0,1:T(1,128)S(1)}, u32[]{:S(2)}) copy-start(s32[256,1]{0,1:T(1,128)S(1)} %compare_select_fusion.8) | copy-start | bytes 3076
  10.2 8.9 copy-start.44
  10.2 0.8 copy-start.43
  10.3 11.6 copy-start.42
  11.0 8.1 collective-permute-start
  16.2 6.3 collective-permute-start.1
  18.4 4.1 copy-start.47
  22.5 15.6 %copy-start.7 = (f32[32,25,128]{2,0,1:T(8,128)S(1)}, f32[32,25,128]{2,0,1:T(8,128)}, u32[]{:S(2)}) copy-start(f32[32,25,128]{2,0,1:T(8,128)} %param.18) | copy-start | bytes 1228804
  22.5 16.6 %copy-start.6 = (f32[32,25,128]{2,0,1:T(8,128)S(1)}, f32[32,25,128]{2,0,1:T(8,128)}, u32[]{:S(2)}) copy-start(f32[32,25,128]{2,0,1:T(8,128)} %param.17) | copy-start | bytes 1228804
  25.3 1.3 copy-start
  25.3 20.8 %copy-start.19 = (s32[32,128]{1,0:T(8,128)S(1)}, s32[32,128]{1,0:T(8,128)}, u32[]{:S(2)}) copy-start(s32[32,128]{1,0:T(8,128)} %param.25) | copy-start | bytes 49156
  26.7 84.6 %all-to-all-start = ((s32[32,1,128]{2,1,0:T(1,128)}), s32[32,1,128]{2,1,0:T(1,128)S(1)}, u32[]{:S(2)}, u32[]{:S(2)}) async-start(s32[32,1,128]{2,1,0:T(1,128)} %bitcast.11), calls=%async_computation | async-start | bytes 32768 | tf_op jit(solution)/shard_map/all_to_all | solution.py:82
  37.9 1016.7 %all-gather.5.cloned.1.call-start = ((), (), s32[]{:S(2)}) async-start(), calls=%async_computation.4 | async-start | bytes 69206016 | tf_op jit(solution)/shard_map/all_gather | solution.py:90
  44.8 42.5 %copy-start.36 = (f32[25,128]{1,0:T(8,128)S(1)}, f32[25,128]{1,0:T(8,128)}, u32[]{:S(2)}) copy-start(f32[25,128]{1,0:T(8,128)} %get-tuple-element.25) | copy-start | bytes 38404
  44.8 49.6 %copy-start.30 = (f32[25,128]{1,0:T(8,128)S(1)}, f32[25,128]{1,0:T(8,128)}, u32[]{:S(2)}) copy-start(f32[25,128]{1,0:T(8,128)} %get-tuple-element.69) | copy-start | bytes 38404
  44.8 49.6 %copy-start.34 = (f32[25,128]{1,0:T(8,128)S(1)}, f32[25,128]{1,0:T(8,128)}, u32[]{:S(2)}) copy-start(f32[25,128]{1,0:T(8,128)} %get-tuple-element.81) | copy-start | bytes 38404
  44.8 49.6 %copy-start.35 = (f32[25,128]{1,0:T(8,128)S(1)}, f32[25,128]{1,0:T(8,128)}, u32[]{:S(2)}) copy-start(f32[25,128]{1,0:T(8,128)} %get-tuple-element.12) | copy-start | bytes 38404
  44.8 49.6 %copy-start.33 = (f32[25,128]{1,0:T(8,128)S(1)}, f32[25,128]{1,0:T(8,128)}, u32[]{:S(2)}) copy-start(f32[25,128]{1,0:T(8,128)} %get-tuple-element.50) | copy-start | bytes 38404
  44.8 49.7 %copy-start.32 = (f32[25,128]{1,0:T(8,128)S(1)}, f32[25,128]{1,0:T(8,128)}, u32[]{:S(2)}) copy-start(f32[25,128]{1,0:T(8,128)} %get-tuple-element.51) | copy-start | bytes 38404
  44.8 49.7 %copy-start.31 = (f32[25,128]{1,0:T(8,128)S(1)}, f32[25,128]{1,0:T(8,128)}, u32[]{:S(2)}) copy-start(f32[25,128]{1,0:T(8,128)} %get-tuple-element.52) | copy-start | bytes 38404
  44.8 49.7 %copy-start.29 = (f32[25,128]{1,0:T(8,128)S(1)}, f32[25,128]{1,0:T(8,128)}, u32[]{:S(2)}) copy-start(f32[25,128]{1,0:T(8,128)} %get-tuple-element.53) | copy-start | bytes 38404
  44.9 49.7 %copy-start.28 = (f32[25,128]{1,0:T(8,128)S(1)}, f32[25,128]{1,0:T(8,128)}, u32[]{:S(2)}) copy-start(f32[25,128]{1,0:T(8,128)} %get-tuple-element.54) | copy-start | bytes 38404
  44.9 49.7 %copy-start.27 = (f32[25,128]{1,0:T(8,128)S(1)}, f32[25,128]{1,0:T(8,128)}, u32[]{:S(2)}) copy-start(f32[25,128]{1,0:T(8,128)} %get-tuple-element.55) | copy-start | bytes 38404
  44.9 49.7 %copy-start.26 = (f32[25,128]{1,0:T(8,128)S(1)}, f32[25,128]{1,0:T(8,128)}, u32[]{:S(2)}) copy-start(f32[25,128]{1,0:T(8,128)} %get-tuple-element.56) | copy-start | bytes 38404
  44.9 49.7 %copy-start.25 = (f32[25,128]{1,0:T(8,128)S(1)}, f32[25,128]{1,0:T(8,128)}, u32[]{:S(2)}) copy-start(f32[25,128]{1,0:T(8,128)} %get-tuple-element.57) | copy-start | bytes 38404
  44.9 49.7 %copy-start.24 = (f32[25,128]{1,0:T(8,128)S(1)}, f32[25,128]{1,0:T(8,128)}, u32[]{:S(2)}) copy-start(f32[25,128]{1,0:T(8,128)} %get-tuple-element.58) | copy-start | bytes 38404
  44.9 49.8 %copy-start.23 = (f32[25,128]{1,0:T(8,128)S(1)}, f32[25,128]{1,0:T(8,128)}, u32[]{:S(2)}) copy-start(f32[25,128]{1,0:T(8,128)} %get-tuple-element.59) | copy-start | bytes 38404
  44.9 49.8 %copy-start.22 = (f32[25,128]{1,0:T(8,128)S(1)}, f32[25,128]{1,0:T(8,128)}, u32[]{:S(2)}) copy-start(f32[25,128]{1,0:T(8,128)} %get-tuple-element.60) | copy-start | bytes 38404
  44.9 49.8 %copy-start.21 = (f32[25,128]{1,0:T(8,128)S(1)}, f32[25,128]{1,0:T(8,128)}, u32[]{:S(2)}) copy-start(f32[25,128]{1,0:T(8,128)} %get-tuple-element.61) | copy-start | bytes 38404
  44.9 49.8 %copy-start.20 = (f32[25,128]{1,0:T(8,128)S(1)}, f32[25,128]{1,0:T(8,128)}, u32[]{:S(2)}) copy-start(f32[25,128]{1,0:T(8,128)} %get-tuple-element.62) | copy-start | bytes 38404
  46.2 45.5 %copy-start.41 = (f32[25,128]{1,0:T(8,128)S(1)}, f32[25,128]{1,0:T(8,128)}, u32[]{:S(2)}) copy-start(f32[25,128]{1,0:T(8,128)} %get-tuple-element.42) | copy-start | bytes 38404
  46.2 46.7 %copy-start.40 = (f32[25,128]{1,0:T(8,128)S(1)}, f32[25,128]{1,0:T(8,128)}, u32[]{:S(2)}) copy-start(f32[25,128]{1,0:T(8,128)} %get-tuple-element.41) | copy-start | bytes 38404
  46.2 48.0 %copy-start.39 = (f32[25,128]{1,0:T(8,128)S(1)}, f32[25,128]{1,0:T(8,128)}, u32[]{:S(2)}) copy-start(f32[25,128]{1,0:T(8,128)} %get-tuple-element.40) | copy-start | bytes 38404
  46.2 48.0 %copy-start.38 = (f32[25,128]{1,0:T(8,128)S(1)}, f32[25,128]{1,0:T(8,128)}, u32[]{:S(2)}) copy-start(f32[25,128]{1,0:T(8,128)} %get-tuple-element.39) | copy-start | bytes 38404
  46.2 48.0 %copy-start.37 = (f32[25,128]{1,0:T(8,128)S(1)}, f32[25,128]{1,0:T(8,128)}, u32[]{:S(2)}) copy-start(f32[25,128]{1,0:T(8,128)} %get-tuple-element.38) | copy-start | bytes 38404
  46.8 48.1 %copy-start.1 = (f32[5,4096]{0,1:T(8,128)S(1)}, f32[5,4096]{0,1:T(8,128)}, u32[]{:S(2)}) copy-start(f32[5,4096]{0,1:T(8,128)} %copy-done) | copy-start | bytes 245764
  47.5 61.5 %copy-start.8 = (s32[4096]{0:T(1024)}, s32[4096]{0:T(1024)S(1)}, u32[]{:S(2)}) copy-start(s32[4096]{0:T(1024)S(1)} %broadcast_clamp_fusion.1) | copy-start | bytes 49156
  134.5 388.9 %copy-start.10 = (s32[4096]{0:T(1024)}, s32[4096]{0:T(1024)S(1)}, u32[]{:S(2)}) copy-start(s32[4096]{0:T(1024)S(1)} %broadcast_clamp_fusion) | copy-start | bytes 49156
  556.6 2.4 copy-start.17
  591.5 3.8 copy-start.12
  595.3 24.7 %copy-start.15 = (f32[4096]{0:T(1024)S(1)}, f32[4096]{0:T(1024)}, u32[]{:S(2)}) copy-start(f32[4096]{0:T(1024)} %param.16) | copy-start | bytes 49156
  608.9 11.9 copy-start.45
  612.1 8.7 collective-permute-start.2
  617.9 6.6 collective-permute-start.3
  620.2 4.3 copy-start.48
  624.0 5.0 copy-start.9
  627.7 1.3 copy-start.2
  629.0 425.6 %copy-start.11 = (s32[4096]{0:T(1024)S(1)}, s32[4096]{0:T(1024)}, u32[]{:S(2)}) copy-start(s32[4096]{0:T(1024)} %copy-done.10) | copy-start | bytes 49156
  1151.6 2.4 copy-start.18
  1186.6 3.8 copy-start.13
  1190.4 23.3 %copy-start.16 = (f32[4096]{0:T(1024)S(1)}, f32[4096]{0:T(1024)}, u32[]{:S(2)}) copy-start(f32[4096]{0:T(1024)} %param.16) | copy-start | bytes 49156
  1204.0 13.4 %copy-start.4 = (f32[4096,5]{0,1:T(8,128)}, f32[4096,5]{0,1:T(8,128)S(1)}, u32[]{:S(2)}) copy-start(f32[4096,5]{0,1:T(8,128)S(1)} %copy.531) | copy-start | bytes 245764
  1204.0 10.5 copy-start.46
  1206.0 8.5 collective-permute-start.4
  1211.7 6.3 collective-permute-start.5
  1213.8 4.2 copy-start.49
Sparse Core Ops, SparseCore 0:
  26.8 432.6 all-gather.2
  629.1 425.4 all-gather.4
where the time goes:
time: 1240 us; the launch traced here: 1230 us
  waiting for transfers between devices  739 us (60%)
  local copies, waits for them, and re-layouts  314 us (25%)
  other arithmetic  95.7 us (8%)
  starting transfers between devices  33.5 us (3%)
  blocking collectives  28.6 us (2%)
  between operations  17.7 us (1%)
    all_gather x2, waiting for transfers between devices, shards(): whole = lax.all_gather(drive_vals, 'dom', axis=1, tiled=True)  738 us
    gather x4, local copies, waits for them, and re-layouts, shards(): whole[:, global_idx]  129 us
    reduce_sum x188, other arithmetic, apply_block(): return jnp.sum(matrix.reshape(nvar, nvar, -1) * vector[None, :, :], axis=1)  63.9 us
    another operation x94, local copies, waits for them, and re-layouts, apply_block(): return jnp.sum(matrix.reshape(nvar, nvar, -1) * vector[None, :, :], axis=1)  43.4 us
    gather x4, local copies, waits for them, and re-layouts, shards(): outgoing = solved[:, ret_slot]  32.6 us
    gather x4, local copies, waits for them, and re-layouts, shards(): drive_vals[:, own_idx]  29.3 us
    all_to_all x2, blocking collectives, shards(): lax.all_to_all(outgoing, 'dom', split_axis=1, concat_axis=1, tiled=True)  28.6 us
    gather x4, local copies, waits for them, and re-layouts, shards(): state_now = pooled[:, cell_src]  27.2 us
  transfers between devices with their start and end apart: 9, of which 5 were waited for; matrix products, arithmetic and copies ran while one was open for 10% of the time, Pallas kernels for 0%

commit v1 on v0

v1 whole, which is shorter than its diff:
```python
import functools

import jax
import jax.numpy as jnp
from jax import lax
from jax.experimental import pallas as pl
from jax.experimental.pallas import tpu as pltpu
from jax.sharding import PartitionSpec as P

SWEEPS = 2
LANES = 128
SUBLANES = 8
MESH = pl.DeviceIdType.MESH


def bcast(row):
    return jnp.broadcast_to(row, (SUBLANES, LANES))


def lane_pick(row, lane):
    return jnp.take_along_axis(bcast(row), lane, axis=1, mode="promise_in_bounds")


def pick_rows(load_row, row_count, row, lane, start, nvar, unroll=8):
    unroll = min(unroll, row_count)

    def body(step, picked):
        picked = list(picked)
        for u in range(unroll):
            r = step * unroll + u
            hit = row == r
            for v in range(nvar):
                picked[v] = jnp.where(hit, lane_pick(load_row(v, r), lane), picked[v])
        return tuple(picked)

    return lax.fori_loop(0, row_count // unroll, body, tuple(start))


def kernel(
    nvar,
    groups,
    domains,
    flow_ref,
    rhs_ref,
    coup_ref,
    piv_hbm,
    low_hbm,
    upp_hbm,
    face_up_ref,
    face_down_ref,
    coef_up_ref,
    coef_down_ref,
    send_idx_ref,
    line_idx_ref,
    ret_idx_ref,
    cell_idx_ref,
    sol_ref,
    drv_ref,
    state,
    drive,
    rhs,
    lines,
    out_buf,
    in_buf,
    piv,
    low,
    upp,
    face_idx,
    inv,
    face_out,
    face_in,
    factor_sem,
    send_sem,
    recv_sem,
    face_send_sem,
    face_recv_sem,
):
    g = lax.axis_index("group")
    d = lax.axis_index("dom")
    rows = state.shape[1]
    blocks = rows // SUBLANES
    length = piv.shape[0]
    above = lax.rem(g + 1, groups)
    below = lax.rem(g + groups - 1, groups)
    zero = jnp.zeros((SUBLANES, LANES), jnp.float32)
    zeros = [zero] * nvar

    factor_copies = [
        pltpu.make_async_copy(src, dst, factor_sem.at[i])
        for i, (src, dst) in enumerate(((piv_hbm, piv), (low_hbm, low), (upp_hbm, upp)))
    ]
    for copy in factor_copies:
        copy.start()

    barrier = pltpu.get_barrier_semaphore()

    def greet(i, carry):
        peer = lax.rem(d + i, domains)
        pl.semaphore_signal(barrier, inc=1, device_id={"dom": peer}, device_id_type=MESH)
        return carry

    lax.fori_loop(1, domains, greet, 0)
    for peer in (above, below):
        pl.semaphore_signal(barrier, inc=1, device_id={"group": peer}, device_id_type=MESH)

    for r in range(rows):
        part = slice(r * LANES, (r + 1) * LANES)
        state[:, r, :] = flow_ref[:, part]
        rhs[:, r, :] = rhs_ref[:, part]

    face_rows = face_up_ref.shape[2] // LANES
    for first, ref in ((0, face_up_ref), (face_rows, face_down_ref)):
        for j in range(face_rows):
            line = ref[0, 0:1, j * LANES : (j + 1) * LANES]
            face_idx[first + j : first + j + 1, :] = line
            face_idx[2 * face_rows + first + j : 2 * face_rows + first + j + 1, :] = line
    faces = face_rows * LANES
    for which, ref in ((0, face_down_ref), (1, face_up_ref)):
        cells = ref[0, 0:1, :]
        number = (lax.broadcasted_iota(jnp.int32, (1, faces), 1) + 1).astype(jnp.float32)
        row_hot = jnp.where(
            lax.broadcasted_iota(jnp.int32, (rows, faces), 0) == (cells >> 7), number, 0.0
        ).astype(jnp.bfloat16)
        lane_hot = jnp.where(
            lax.broadcasted_iota(jnp.int32, (LANES, faces), 0) == (cells & 127), 1.0, 0.0
        ).astype(jnp.bfloat16)
        found = lax.dot_general(
            row_hot, lane_hot, (((1,), (1,)), ((), ())), preferred_element_type=jnp.float32
        )
        inv[which] = found.astype(jnp.int32)

    def state_row(v, r):
        return state[v, pl.ds(r, 1), :]

    def drive_row(v, r):
        return drive[v, pl.ds(r, 1), :]

    def lines_row(v, r):
        return lines[v, pl.ds(r, 1), :]

    def pick_faces(turn):
        index = face_idx[...]
        picked = pick_rows(state_row, rows, index >> 7, index & 127, zeros, nvar)
        for v in range(nvar):
            face_out[turn, 0, v, 0:face_rows, :] = picked[v][0:face_rows]
            face_out[turn, 1, v, 0:face_rows, :] = picked[v][face_rows : 2 * face_rows]

    def face_copy(turn, way):
        return pltpu.make_async_remote_copy(
            src_ref=face_out.at[turn, way],
            dst_ref=face_in.at[turn, way],
            send_sem=face_send_sem.at[turn, way],
            recv_sem=face_recv_sem.at[turn, way],
            device_id={"group": above if way == 0 else below},
            device_id_type=MESH,
        )

    edge = (g == 0, g == groups - 1)

    def drive_term(turn, write):
        lane_ids = lax.broadcasted_iota(jnp.int32, (rows, LANES), 1)
        row_ids = lax.broadcasted_iota(jnp.int32, (rows, LANES), 0)
        first = (lane_ids == 0) & (row_ids == 0)
        last = (lane_ids == LANES - 1) & (row_ids == rows - 1)
        coup = coup_ref[...]
        for v in range(nvar):
            x = state[v]
            left = pltpu.roll(x, 1, 1)
            left = jnp.where(lane_ids == 0, pltpu.roll(left, 1, 0), left)
            right = pltpu.roll(x, LANES - 1, 1)
            right = jnp.where(lane_ids == LANES - 1, pltpu.roll(right, rows - 1, 0), right)
            beside = jnp.where(first, 0.0, left) + jnp.where(last, 0.0, right)
            drive[v] = rhs[v] + coup * beside
        for way in range(2):
            face_copy(turn, way).wait_recv()
        for way, coef_ref in ((0, coef_down_ref), (1, coef_up_ref)):
            for v in range(nvar):
                for j in range(face_rows):
                    coef = coef_ref[0, 0:1, j * LANES : (j + 1) * LANES]
                    value = coef * face_in[turn, way, v, j : j + 1, :]
                    face_in[turn, way, v, j : j + 1, :] = jnp.where(edge[way], 0.0, value)

        def block(b, carry):
            part = pl.ds(pl.multiple_of(b * SUBLANES, SUBLANES), SUBLANES)
            total = [drive[v, part, :] for v in range(nvar)]
            for way in range(2):
                item = inv[way, part, :] - 1
                row, lane = item >> 7, item & 127
                for v in range(nvar):
                    add = zero
                    for j in range(face_rows):
                        value = face_in[turn, way, v, j : j + 1, :]
                        add = jnp.where(row == j, lane_pick(value, lane), add)
                    total[v] = total[v] + add
            for v in range(nvar):
                write(v, b, part, total[v])
            return carry

        lax.fori_loop(0, blocks, block, 0)

    def write_drive(v, b, part, value):
        drive[v, part, :] = value

    def block_copy(phase, peer, slot, sem):
        return pltpu.make_async_remote_copy(
            src_ref=out_buf.at[phase, peer],
            dst_ref=in_buf.at[phase, slot],
            send_sem=send_sem.at[phase, peer],
            recv_sem=recv_sem.at[phase, sem],
            device_id={"dom": peer},
            device_id_type=MESH,
        )

    def exchange(phase, load_row, index_ref):
        def block(b, carry):
            start = pl.multiple_of(b * SUBLANES, SUBLANES)
            index = index_ref[pl.ds(start, SUBLANES), :]
            picked = pick_rows(load_row, rows, index >> 7, index & 127, zeros, nvar)
            for v in range(nvar):
                for s in range(SUBLANES):
                    out_buf[phase, start + s, v : v + 1, :] = picked[v][s : s + 1]
            return carry

        lax.fori_loop(0, domains // SUBLANES, block, 0)

        def send(i, carry):
            block_copy(phase, lax.rem(d + i, domains), d, d).start()
            return carry

        lax.fori_loop(1, domains, send, 0)

    def receive(phase):
        def wait(i, carry):
            peer = lax.rem(d + i, domains)
            block_copy(phase, peer, peer, peer).wait_recv()
            return carry

        lax.fori_loop(1, domains, wait, 0)

    def merge(phase, load_row, index_ref, out):
        def pool_row(v, r):
            return in_buf[phase, r, v : v + 1, :]

        def own(b, carry):
            part = pl.ds(pl.multiple_of(b * SUBLANES, SUBLANES), SUBLANES)
            index = index_ref[part, :]
            row, lane = (index >> 7) - domains, index & 127
            picked = pick_rows(load_row, rows, row, lane, zeros, nvar)
            for v in range(nvar):
                out[v, part, :] = picked[v]
            return carry

        def pool(b, carry):
            part = pl.ds(pl.multiple_of(b * SUBLANES, SUBLANES), SUBLANES)
            index = index_ref[part, :]
            begin = [out[v, part, :] for v in range(nvar)]
            picked = pick_rows(pool_row, domains, index >> 7, index & 127, begin, nvar)
            for v in range(nvar):
                out[v, part, :] = picked[v]
            return carry

        lax.fori_loop(0, blocks, own, 0)
        receive(phase)
        lax.fori_loop(0, blocks, pool, 0)

    def apply_block(ref, p, vector):
        result = []
        for a in range(nvar):
            terms = [
                bcast(ref[p, a * nvar + b : a * nvar + b + 1, :]) * vector[b] for b in range(nvar)
            ]
            result.append((terms[0] + terms[1]) + (terms[2] + terms[3]) + terms[4])
        return result

    def solve():
        def row_of(p):
            return [bcast(lines[v, pl.ds(p, 1), :]) for v in range(nvar)]

        def put(p, values):
            for v in range(nvar):
                lines[v, pl.ds(p, 1), :] = values[v][0:1]

        first = apply_block(piv, 0, row_of(0))
        put(0, first)

        def forward(p, previous):
            term = apply_block(low, p, previous)
            reduced = [q - t for q, t in zip(row_of(p), term)]
            result = apply_block(piv, p, reduced)
            put(p, result)
            return tuple(result)

        last = lax.fori_loop(1, length, forward, tuple(first))

        def backward(i, later):
            p = length - 2 - i
            term = apply_block(upp, p, later)
            result = [y - t for y, t in zip(row_of(p), term)]
            put(p, result)
            return tuple(result)

        lax.fori_loop(0, length - 1, backward, last)

    pick_faces(0)
    pl.semaphore_wait(barrier, domains + 1)
    for way in range(2):
        face_copy(0, way).start()
    for copy in factor_copies:
        copy.wait()

    for sweep in range(SWEEPS):
        drive_term(sweep, write_drive)
        exchange(2 * sweep, drive_row, send_idx_ref)
        merge(2 * sweep, drive_row, line_idx_ref, lines)
        solve()
        exchange(2 * sweep + 1, lines_row, ret_idx_ref)
        merge(2 * sweep + 1, lines_row, cell_idx_ref, state)
        pick_faces(sweep + 1)
        for way in range(2):
            face_copy(sweep + 1, way).start()
    for r in range(rows):
        sol_ref[:, r * LANES : (r + 1) * LANES] = state[:, r, :]
    drive_term(SWEEPS, write_drive)
    for r in range(rows):
        drv_ref[:, r * LANES : (r + 1) * LANES] = drive[:, r, :]

    for turn in range(SWEEPS + 1):
        for way in range(2):
            face_copy(turn, way).wait_send()

    def drain(i, carry):
        for phase in range(2 * SWEEPS):
            block_copy(phase, lax.rem(d + i, domains), d, d).wait_send()
        return carry

    lax.fori_loop(1, domains, drain, 0)


def shards(*args):
    (flow_state, right_side, coupling, pivot_inv, lower_blocks, upper_blocks, face_up, face_down,
     coef_up, coef_down, send_cell, line_src, ret_slot, cell_src) = args
    nvar, cell_count = flow_state.shape
    rows = cell_count // LANES
    groups, domains = lax.axis_size("group"), lax.axis_size("dom")
    face_rows = face_up.shape[2] // LANES
    vmem = pl.BlockSpec(memory_space=pltpu.VMEM)
    hbm = pl.BlockSpec(memory_space=pl.ANY)
    f32, dma = jnp.float32, pltpu.SemaphoreType.DMA
    grid_field = pltpu.VMEM((nvar, rows, LANES), f32)
    pool = pltpu.VMEM((2 * SWEEPS, domains, nvar, LANES), f32)
    turns = SWEEPS + 1
    out = jax.ShapeDtypeStruct(flow_state.shape, f32)
    return pl.pallas_call(
        functools.partial(kernel, nvar, groups, domains),
        out_shape=(out, out),
        in_specs=[vmem] * 3 + [hbm] * 3 + [vmem] * 8,
        out_specs=(vmem, vmem),
        scratch_shapes=[
            grid_field,
            grid_field,
            grid_field,
            grid_field,
            pool,
            pool,
            pltpu.VMEM(pivot_inv.shape, f32),
            pltpu.VMEM(pivot_inv.shape, f32),
            pltpu.VMEM(pivot_inv.shape, f32),
            pltpu.VMEM((SUBLANES, LANES), jnp.int32),
            pltpu.VMEM((2, rows, LANES), jnp.int32),
            pltpu.VMEM((turns, 2, nvar, SUBLANES, LANES), f32),
            pltpu.VMEM((turns, 2, nvar, SUBLANES, LANES), f32),
            dma((3,)),
            dma((2 * SWEEPS, domains)),
            dma((2 * SWEEPS, domains)),
            dma((turns, 2)),
            dma((turns, 2)),
        ],
        compiler_params=pltpu.CompilerParams(collective_id=0, has_side_effects=True),
        name="relax",
    )(flow_state, right_side, coupling.reshape(rows, LANES), pivot_inv, lower_blocks, upper_blocks,
      face_up, face_down, coef_up, coef_down, send_cell, line_src, ret_slot,
      cell_src.reshape(rows, LANES))


def solution(mesh):
    both = ("group", "dom")
    lead, face = P(None, both), P("group", "dom", None)
    return jax.shard_map(
        shards,
        mesh=mesh,
        in_specs=(lead, lead, P(both)) + (P(None, None, both),) * 3 + (face,) * 4
        + (lead, lead, lead, P(both)),
        out_specs=(lead, lead),
        check_vma=False,
    )
```

time: 1240 us -> 74 us (0.06)
  waiting for transfers between devices: 739 us -> 0 us
  local copies, waits for them, and re-layouts: 314 us -> 6.43 us
  other arithmetic: 95.7 us -> 0 us
  Pallas kernels: 0 us -> 66.7 us
  starting transfers between devices: 33.5 us -> 0 us
  blocking collectives: 28.6 us -> 0 us
  between operations: 17.7 us -> 0.66 us
    all_gather x2 -> x0, waiting for transfers between devices: 738 us -> none  [shards(): whole = lax.all_gather(drive_vals, 'dom', axis=1, tiled=True)]
    gather x23 -> x0, local copies, waits for them, and re-layouts: 248 us -> none  [the longest x4 129 us: shards(): whole[:, global_idx]]
    pallas_call x0 -> x1, Pallas kernels: none -> 66.7 us  [shards(): pl.pallas_call(functools.partial(kernel, nvar, groups, domains), out_shap...]
    reduce_sum x188 -> x0, other arithmetic: 63.9 us -> none  [apply_block(): return jnp.sum(matrix.reshape(nvar, nvar, -1) * vector[None, :, :], axis=1)]
    another operation x98 -> x0, local copies, waits for them, and re-layouts: 44.7 us -> none  [the longest x94 43.4 us: apply_block(): return jnp.sum(matrix.reshape(nvar, nvar, -1) * vector[None, :, :], axis=1)]
    all_to_all x2 -> x0, blocking collectives: 28.6 us -> none  [shards(): lax.all_to_all(outgoing, 'dom', split_axis=1, concat_axis=1, tiled=True)]
    ppermute x6 -> x0, starting transfers between devices: 22 us -> none  [shifted(): return lax.ppermute(block, axis, route)]
    scatter-add x6 -> x0, other arithmetic: 17.7 us -> none  [the longest x3 8.88 us: drive_term(): total = total.at[:, down_cells].add(down_coef[None, :] * from_below)]
  transfers between devices with their start and end apart: 9 -> 0, of which waited for: 5 -> 0; matrix products, arithmetic and copies ran while one was open for 10% -> 0% of each run, Pallas kernels for 0% -> 0%
where the time goes in v1:
time: 74 us; the launch traced here: 73.8 us
  Pallas kernels  66.7 us (90%)
  local copies, waits for them, and re-layouts  6.43 us (9%)
    pallas_call x1, Pallas kernels, shards(): pl.pallas_call(functools.partial(kernel, nvar, groups, domains), out_shap...  66.7 us
    unnamed x11, local copies, waits for them, and re-layouts  6.43 us

profile of v1, /device:TPU:1, one launch (start us, length us, event | category | flops | bytes accessed | tf_op | source)
XLA Modules:
  0.0 73.8 jit_solution(3534690714193477311)
XLA Ops:
  0.6 0.0 copy-start
  0.6 2.1 %copy.16.piv_hbm = f32[32,25,128]{2,1,0:T(8,128)} copy(f32[32,25,128]{2,0,1:T(8,128)} %param.17) | data formatting | bytes 819200 | tf_op args[3]
  2.7 0.0 copy-done
  2.7 0.0 copy-start.1
  2.7 1.0 %copy.17.low_hbm = f32[32,25,128]{2,1,0:T(8,128)} copy(f32[32,25,128]{2,0,1:T(8,128)S(1)} %copy-done) | data formatting | bytes 819200 | tf_op args[4]
  3.8 0.0 copy-done.1
  3.8 1.1 %copy.18.upp_hbm = f32[32,25,128]{2,1,0:T(8,128)} copy(f32[32,25,128]{2,0,1:T(8,128)S(1)} %copy-done.1) | data formatting | bytes 819200 | tf_op args[5]
  4.8 66.7 %relax.1 = (f32[5,4096]{1,0:T(8,128)}, f32[5,4096]{1,0:T(8,128)}) custom-call(f32[5,4096]{1,0:T(8,128)} %flow_ref.1, f32[5,4096]{1,0:T(8,128)} %rhs_ref.1, f32[32,128]{1,0:T(8,128)} %bitcast.2, f32[32,25,128]{2,1,0:T(8,128)} %copy.16.piv_hbm, f32[32,25,128]{2,1,0:T(8,128)} %copy.17.low_hbm, f32[32,25,128]{2,1,0:T(8,128)} %copy.18.upp_hbm, ...), custom_call_target="tpu_custom_call" | custom-call | tf_op jit(solution)/shard_map/relax/pallas_call | solution.py:353
  71.5 0.0 copy-start.2
  71.5 1.6 %copy.21 = f32[5,4096]{1,0:T(8,128)} copy(f32[5,4096]{1,0:T(8,128)} %get-tuple-element.4) | data formatting | bytes 163840
  73.1 0.0 copy-done.2
  73.1 0.7 copy.22
Async XLA Ops:
  0.6 2.1 %copy-start = (f32[32,25,128]{2,0,1:T(8,128)S(1)}, f32[32,25,128]{2,0,1:T(8,128)}, u32[]{:S(2)}) copy-start(f32[32,25,128]{2,0,1:T(8,128)} %param.18) | copy-start | bytes 1228804
  2.7 1.0 %copy-start.1 = (f32[32,25,128]{2,0,1:T(8,128)S(1)}, f32[32,25,128]{2,0,1:T(8,128)}, u32[]{:S(2)}) copy-start(f32[32,25,128]{2,0,1:T(8,128)} %param.19) | copy-start | bytes 1228804
  71.5 1.6 %copy-start.2 = (f32[5,4096]{1,0:T(8,128)S(1)}, f32[5,4096]{1,0:T(8,128)}, u32[]{:S(2)}) copy-start(f32[5,4096]{1,0:T(8,128)} %get-tuple-element.5) | copy-start | bytes 245764

commit v2 on v1

v2 whole, which is shorter than its diff:
```python
import functools

import jax
import jax.numpy as jnp
from jax import lax
from jax.experimental import pallas as pl
from jax.experimental.pallas import tpu as pltpu
from jax.sharding import PartitionSpec as P

SWEEPS = 2
LANES = 128
SUBLANES = 8
UNROLL = 4
MESH = pl.DeviceIdType.MESH


def bcast(row):
    return jnp.broadcast_to(row, (SUBLANES, LANES))


def lane_pick(row, lane):
    return jnp.take_along_axis(row, lane, axis=1, mode="promise_in_bounds")


def ring_order(i):
    return i + i // 2 - 2 * (i // 3)


NEAR_FIRST = (0, 1, 7, 2, 6, 3, 5, 4)


def pick_row(picked, load_row, r, row, lane, nvar):
    hits = [one == r for one in row]
    for v in range(nvar):
        values = bcast(load_row(v, r))
        for b, hit in enumerate(hits):
            at = b * nvar + v
            picked[at] = jnp.where(hit, lane_pick(values, lane[b]), picked[at])


def kernel(
    nvar,
    groups,
    domains,
    flow_hbm,
    rhs_hbm,
    coup_hbm,
    piv_hbm,
    low_hbm,
    upp_hbm,
    face_up_hbm,
    face_down_hbm,
    coef_up_hbm,
    coef_down_hbm,
    send_idx_hbm,
    line_idx_hbm,
    ret_idx_hbm,
    cell_idx_hbm,
    sol_hbm,
    drv_hbm,
    flow_in,
    rhs_in,
    coup_ref,
    piv,
    low,
    upp,
    face_up_ref,
    face_down_ref,
    coef_up_ref,
    coef_down_ref,
    send_idx_ref,
    line_idx_ref,
    ret_idx_ref,
    cell_idx_ref,
    state,
    drive,
    rhs,
    lines,
    out_buf,
    in_buf,
    face_idx,
    inv,
    face_out,
    face_in,
    fetch_sem,
    result_sem,
    send_sem,
    recv_sem,
    face_send_sem,
    face_recv_sem,
):
    g = lax.axis_index("group")
    d = lax.axis_index("dom")
    rows = state.shape[1]
    blocks = rows // SUBLANES
    length = piv.shape[1]
    above = lax.rem(g + 1, groups)
    below = lax.rem(g + groups - 1, groups)
    zero = jnp.zeros((SUBLANES, LANES), jnp.float32)
    tall = domains // SUBLANES
    ring, place = d // SUBLANES, lax.rem(d, SUBLANES)

    sources = (flow_hbm, rhs_hbm, coup_hbm, piv_hbm, low_hbm, upp_hbm, face_up_hbm, face_down_hbm,
               coef_up_hbm, coef_down_hbm, send_idx_hbm, line_idx_hbm, ret_idx_hbm, cell_idx_hbm)
    targets = (flow_in, rhs_in, coup_ref, piv, low, upp, face_up_ref, face_down_ref,
               coef_up_ref, coef_down_ref, send_idx_ref, line_idx_ref, ret_idx_ref, cell_idx_ref)
    fetches = [
        pltpu.make_async_copy(src, dst, fetch_sem.at[i])
        for i, (src, dst) in enumerate(zip(sources, targets))
    ]
    late = (3, 4, 5)
    early = [i for i in range(len(fetches)) if i not in late]

    barrier = pltpu.get_barrier_semaphore()

    def greet(i, carry):
        peer = lax.rem(d + i, domains)
        pl.semaphore_signal(barrier, inc=1, device_id={"dom": peer}, device_id_type=MESH)
        return carry

    for peer in (above, below):
        pl.semaphore_signal(barrier, inc=1, device_id={"group": peer}, device_id_type=MESH)
    for i in early:
        fetches[i].start()
    lax.fori_loop(1, domains, greet, 0)
    for i in late:
        fetches[i].start()
    for i in early:
        fetches[i].wait()

    for r in range(rows):
        part = slice(r * LANES, (r + 1) * LANES)
        state[:, r, :] = flow_in[:, part]
        rhs[:, r, :] = rhs_in[:, part]

    face_rows = face_up_ref.shape[2] // LANES
    for first, ref in ((0, face_up_ref), (face_rows, face_down_ref)):
        for j in range(face_rows):
            line = ref[0, 0:1, j * LANES : (j + 1) * LANES]
            face_idx[first + j : first + j + 1, :] = line
            face_idx[2 * face_rows + first + j : 2 * face_rows + first + j + 1, :] = line
    faces = face_rows * LANES

    def state_row(v, r):
        return state[v, pl.ds(r, 1), :]

    def drive_row(v, r):
        return drive[v, pl.ds(r, 1), :]

    def lines_row(v, r):
        return lines[v, pl.ds(r, 1), :]

    def pick_block(load_row, index):
        picked = [zero] * nvar
        for r in range(rows):
            pick_row(picked, load_row, r, [index >> 7], [index & 127], nvar)
        return picked

    def pick_faces(turn):
        picked = pick_block(state_row, face_idx[...])
        for v in range(nvar):
            face_out[turn, 0, v, :, :] = picked[v][0:face_rows]
            face_out[turn, 1, v, :, :] = picked[v][face_rows : 2 * face_rows]

    def face_copy(turn, way):
        return pltpu.make_async_remote_copy(
            src_ref=face_out.at[turn, way],
            dst_ref=face_in.at[turn, way],
            send_sem=face_send_sem.at[turn, way],
            recv_sem=face_recv_sem.at[turn, way],
            device_id={"group": above if way == 0 else below},
            device_id_type=MESH,
        )

    edge = (g == 0, g == groups - 1)

    def drive_local():
        lane_ids = lax.broadcasted_iota(jnp.int32, (rows, LANES), 1)
        row_ids = lax.broadcasted_iota(jnp.int32, (rows, LANES), 0)
        first = (lane_ids == 0) & (row_ids == 0)
        last = (lane_ids == LANES - 1) & (row_ids == rows - 1)
        coup = coup_ref[...]
        for v in range(nvar):
            x = state[v]
            left = pltpu.roll(x, 1, 1)
            left = jnp.where(lane_ids == 0, pltpu.roll(left, 1, 0), left)
            right = pltpu.roll(x, LANES - 1, 1)
            right = jnp.where(lane_ids == LANES - 1, pltpu.roll(right, rows - 1, 0), right)
            beside = jnp.where(first, 0.0, left) + jnp.where(last, 0.0, right)
            drive[v] = rhs[v] + coup * beside

    def drive_faces(turn):
        for way in range(2):
            face_copy(turn, way).wait_recv()
        tables = []
        for way, coef_ref in ((0, coef_down_ref), (1, coef_up_ref)):
            for j in range(face_rows):
                coef = coef_ref[0, 0:1, j * LANES : (j + 1) * LANES]
                for v in range(nvar):
                    value = coef * face_in[turn, way, v, j : j + 1, :]
                    tables.append(bcast(jnp.where(edge[way], 0.0, value)))
        for b in range(blocks):
            part = slice(b * SUBLANES, (b + 1) * SUBLANES)
            items = [inv[way, part, :] - 1 for way in range(2)]
            for v in range(nvar):
                total = drive[v, part, :]
                for way in range(2):
                    add = zero
                    for j in range(face_rows):
                        table = tables[(way * face_rows + j) * nvar + v]
                        add = jnp.where(
                            (items[way] >> 7) == j, lane_pick(table, items[way] & 127), add
                        )
                    total = total + add
                drive[v, part, :] = total

    def block_copy(phase, peer, slot):
        return pltpu.make_async_remote_copy(
            src_ref=out_buf.at[phase, peer],
            dst_ref=in_buf.at[phase, slot],
            send_sem=send_sem.at[phase, peer],
            recv_sem=recv_sem.at[phase, slot],
            device_id={"dom": peer},
            device_id_type=MESH,
        )

    def exchange(phase, load_row, index_ref):
        def one_ring(i, carry):
            offset = ring_order(tall - 1 - i)
            start = pl.multiple_of(lax.rem(ring + offset, tall) * SUBLANES, SUBLANES)
            picked = pick_block(load_row, index_ref[pl.ds(start, SUBLANES), :])
            for s in range(SUBLANES):
                for v in range(nvar):
                    out_buf[phase, start + s, v : v + 1, :] = picked[v][s : s + 1]
            for step in NEAR_FIRST[:0:-1]:
                block_copy(phase, start + lax.rem(place + step, SUBLANES), d).start()

            @pl.when(offset != 0)
            def _():
                block_copy(phase, start + place, d).start()

            return carry

        lax.fori_loop(0, tall, one_ring, 0)

    def merge(phase, load_row, index_ref, out):
        parts = [slice(b * SUBLANES, (b + 1) * SUBLANES) for b in range(blocks)]
        index = [index_ref[part, :] for part in parts]
        row, lane = [one >> 7 for one in index], [one & 127 for one in index]
        own_row = [one - domains for one in row]

        def pool_row(v, r):
            return in_buf[phase, r, v : v + 1, :]

        def own(step, picked):
            picked = list(picked)
            for u in range(SUBLANES):
                pick_row(picked, load_row, step * SUBLANES + u, own_row, lane, nvar)
            return tuple(picked)

        def pool(i, picked):
            picked = list(picked)
            offset = ring_order(i)
            start = lax.rem(ring + offset, tall) * SUBLANES
            for step in NEAR_FIRST:
                r = start + lax.rem(place + step, SUBLANES)
                if step:
                    block_copy(phase, r, r).wait_recv()
                else:

                    @pl.when(offset != 0)
                    def _():
                        block_copy(phase, r, r).wait_recv()

                pick_row(picked, pool_row, r, row, lane, nvar)
            return tuple(picked)

        picked = lax.fori_loop(0, blocks, own, tuple([zero] * (nvar * blocks)))
        picked = lax.fori_loop(0, tall, pool, picked)
        for b, part in enumerate(parts):
            for v in range(nvar):
                out[v, part, :] = picked[b * nvar + v]

    def apply_block(ref, p, vector):
        result = []
        for a in range(nvar):
            terms = [
                bcast(ref[a * nvar + b, pl.ds(p, 1), :]) * vector[b] for b in range(nvar)
            ]
            result.append((terms[0] + terms[1]) + (terms[2] + terms[3]) + terms[4])
        return result

    def solve():
        def row_of(p):
            return [bcast(lines[v, pl.ds(p, 1), :]) for v in range(nvar)]

        def put(p, values):
            for v in range(nvar):
                lines[v, pl.ds(p, 1), :] = values[v][0:1]

        def forward(step, previous):
            for u in range(UNROLL):
                p = step * UNROLL + u
                term = apply_block(low, p, previous)
                reduced = [q - t for q, t in zip(row_of(p), term)]
                previous = apply_block(piv, p, reduced)
                put(p, previous)
            return tuple(previous)

        def backward(step, later):
            for u in range(UNROLL):
                p = length - 1 - step * UNROLL - u
                term = apply_block(upp, p, later)
                later = [y - t for y, t in zip(row_of(p), term)]
                put(p, later)
            return tuple(later)

        ends = tuple([zero] * nvar)
        lax.fori_loop(0, length // UNROLL, forward, ends)
        lax.fori_loop(0, length // UNROLL, backward, ends)

    pick_faces(0)
    drive_local()
    for which, ref in ((0, face_down_ref), (1, face_up_ref)):
        cells = ref[0, 0:1, :]
        number = (lax.broadcasted_iota(jnp.int32, (1, faces), 1) + 1).astype(jnp.float32)
        row_hot = jnp.where(
            lax.broadcasted_iota(jnp.int32, (rows, faces), 0) == (cells >> 7), number, 0.0
        ).astype(jnp.bfloat16)
        lane_hot = jnp.where(
            lax.broadcasted_iota(jnp.int32, (LANES, faces), 0) == (cells & 127), 1.0, 0.0
        ).astype(jnp.bfloat16)
        found = lax.dot_general(
            row_hot, lane_hot, (((1,), (1,)), ((), ())), preferred_element_type=jnp.float32
        )
        inv[which] = found.astype(jnp.int32)

    pl.semaphore_wait(barrier, domains + 1)
    for way in range(2):
        face_copy(0, way).start()

    for sweep in range(SWEEPS):
        if sweep:
            drive_local()
        drive_faces(sweep)
        exchange(2 * sweep, drive_row, send_idx_ref)
        merge(2 * sweep, drive_row, line_idx_ref, lines)
        if sweep == 0:
            for i in late:
                fetches[i].wait()
        solve()
        exchange(2 * sweep + 1, lines_row, ret_idx_ref)
        merge(2 * sweep + 1, lines_row, cell_idx_ref, state)
        pick_faces(sweep + 1)
        for way in range(2):
            face_copy(sweep + 1, way).start()
    sol_copy = pltpu.make_async_copy(state, sol_hbm, result_sem.at[0])
    sol_copy.start()
    drive_local()
    drive_faces(SWEEPS)
    drv_copy = pltpu.make_async_copy(drive, drv_hbm, result_sem.at[1])
    drv_copy.start()

    for turn in range(SWEEPS + 1):
        for way in range(2):
            face_copy(turn, way).wait_send()

    def drain(i, carry):
        for phase in range(2 * SWEEPS):
            block_copy(phase, lax.rem(d + i, domains), d).wait_send()
        return carry

    lax.fori_loop(1, domains, drain, 0)
    sol_copy.wait()
    drv_copy.wait()


def shards(*args):
    (flow_state, right_side, coupling, pivot_inv, lower_blocks, upper_blocks, face_up, face_down,
     coef_up, coef_down, send_cell, line_src, ret_slot, cell_src) = args
    nvar, cell_count = flow_state.shape
    rows = cell_count // LANES
    groups, domains = lax.axis_size("group"), lax.axis_size("dom")
    face_rows = face_up.shape[2] // LANES
    hbm = pl.BlockSpec(memory_space=pl.ANY)
    f32, dma = jnp.float32, pltpu.SemaphoreType.DMA
    operands = (
        flow_state, right_side, coupling.reshape(rows, LANES),
        jnp.transpose(pivot_inv, (1, 0, 2)), jnp.transpose(lower_blocks, (1, 0, 2)),
        jnp.transpose(upper_blocks, (1, 0, 2)),
        face_up, face_down, coef_up, coef_down, send_cell, line_src, ret_slot,
        cell_src.reshape(rows, LANES),
    )
    field = (nvar, rows, LANES)
    grid_field = pltpu.VMEM(field, f32)
    pool = pltpu.VMEM((2 * SWEEPS, domains, nvar, LANES), f32)
    turns = SWEEPS + 1
    faces = pltpu.VMEM((turns, 2, nvar, face_rows, LANES), f32)
    out = jax.ShapeDtypeStruct(field, f32)
    sol, drv = pl.pallas_call(
        functools.partial(kernel, nvar, groups, domains),
        out_shape=(out, out),
        in_specs=[hbm] * len(operands),
        out_specs=(hbm, hbm),
        scratch_shapes=[pltpu.VMEM(x.shape, x.dtype) for x in operands] + [
            grid_field,
            grid_field,
            grid_field,
            grid_field,
            pool,
            pool,
            pltpu.VMEM((SUBLANES, LANES), jnp.int32),
            pltpu.VMEM((2, rows, LANES), jnp.int32),
            faces,
            faces,
            dma((len(operands),)),
            dma((2,)),
            dma((2 * SWEEPS, domains)),
            dma((2 * SWEEPS, domains)),
            dma((turns, 2)),
            dma((turns, 2)),
        ],
        compiler_params=pltpu.CompilerParams(collective_id=0, has_side_effects=True),
        name="relax",
    )(*operands)
    return sol.reshape(nvar, cell_count), drv.reshape(nvar, cell_count)


def solution(mesh):
    both = ("group", "dom")
    lead, face = P(None, both), P("group", "dom", None)
    return jax.shard_map(
        shards,
        mesh=mesh,
        in_specs=(lead, lead, P(both)) + (P(None, None, both),) * 3 + (face,) * 4
        + (lead, lead, lead, P(both)),
        out_specs=(lead, lead),
        check_vma=False,
    )
```

time: 74 us -> 62.4 us (0.84)
  Pallas kernels: 66.7 us -> 59.9 us
  local copies, waits for them, and re-layouts: 6.43 us -> 1.73 us
    pallas_call x1, Pallas kernels: 66.7 us -> 59.9 us  [shards(): pl.pallas_call(functools.partial(kernel, nvar, groups, domains), out_shap...]
    unnamed x11 -> x0, local copies, waits for them, and re-layouts: 6.43 us -> none
    reshape x0 -> x1, local copies, waits for them, and re-layouts: none -> 1.73 us  [shards(): return (sol.reshape(nvar, cell_count), drv.reshape(nvar, cell_count))]
where the time goes in v2:
time: 62.4 us; the launch traced here: 62.3 us
  Pallas kernels  59.9 us (96%)
  local copies, waits for them, and re-layouts  1.73 us (3%)
  between operations  0.64 us (1%)
    pallas_call x1, Pallas kernels, shards(): pl.pallas_call(functools.partial(kernel, nvar, groups, domains), out_shap...  59.9 us
    reshape x1, local copies, waits for them, and re-layouts, shards(): return (sol.reshape(nvar, cell_count), drv.reshape(nvar, cell_count))  1.73 us

profile of v2, /device:TPU:1, one launch (start us, length us, event | category | flops | bytes accessed | tf_op | source)
XLA Modules:
  0.0 62.3 jit_solution(8466302716651323219)
XLA Ops:
  0.6 59.9 %relax.1 = (f32[5,32,128]{2,1,0:T(8,128)}, f32[5,32,128]{2,1,0:T(8,128)}) custom-call(f32[5,4096]{1,0:T(8,128)} %flow_hbm.1, f32[5,4096]{1,0:T(8,128)} %rhs_hbm.1, f32[32,128]{1,0:T(8,128)} %bitcast.16, f32[25,32,128]{2,1,0:T(8,128)} %bitcast.11, f32[25,32,128]{2,1,0:T(8,128)} %bitcast.12, f32[25,32,128]{2,1,0:T(8,128)} %bitcast.13, ...), custom_call_target="tpu_custom_call" | custom-call | tf_op jit(solution)/shard_map/relax/pallas_call | solution.py:400
  60.6 1.7 %copy_bitcast_fusion = (f32[5,4096]{1,0:T(8,128)}, f32[5,4096]{1,0:T(8,128)}) fusion(f32[1,5,32,128]{3,2,1,0:T(8,128)} %bitcast.15, f32[1,5,32,128]{3,2,1,0:T(8,128)} %bitcast.14), kind=kLoop, calls=%fused_computation | loop fusion | bytes 327680 | tf_op jit(solution)/shard_map/reshape | solution.py:426

commit v3 on v2

--- a/solution.py
+++ b/solution.py
@@ -10,7 +10,7 @@
 SWEEPS = 2
 LANES = 128
 SUBLANES = 8
-UNROLL = 4
+UNROLL = 8
 MESH = pl.DeviceIdType.MESH
 
 
@@ -22,11 +22,7 @@
     return jnp.take_along_axis(row, lane, axis=1, mode="promise_in_bounds")
 
 
-def ring_order(i):
-    return i + i // 2 - 2 * (i // 3)
-
-
-NEAR_FIRST = (0, 1, 7, 2, 6, 3, 5, 4)
+RINGS = (2, 1, 3, 0)
 
 
 def pick_row(picked, load_row, r, row, lane, nvar):
@@ -56,8 +52,8 @@
     line_idx_hbm,
     ret_idx_hbm,
     cell_idx_hbm,
-    sol_hbm,
-    drv_hbm,
+    sol_out,
+    drv_out,
     flow_in,
     rhs_in,
     coup_ref,
@@ -78,6 +74,8 @@
     lines,
     out_buf,
     in_buf,
+    send_map,
+    ret_map,
     face_idx,
     inv,
     face_out,
@@ -157,10 +155,21 @@
         return picked
 
     def pick_faces(turn):
-        picked = pick_block(state_row, face_idx[...])
+        half = rows // 2
+        index = face_idx[...]
+        low_part = lax.broadcasted_iota(jnp.int32, (SUBLANES, LANES), 0) < SUBLANES // 2
+        row, lane = jnp.where(low_part, index >> 7, (index >> 7) - half), index & 127
+        picked = [zero] * nvar
+        for r in range(half):
+            hit = row == r
+            for v in range(nvar):
+                values = jnp.where(low_part, bcast(state_row(v, r)), bcast(state_row(v, r + half)))
+                picked[v] = jnp.where(hit, lane_pick(values, lane), picked[v])
         for v in range(nvar):
-            face_out[turn, 0, v, :, :] = picked[v][0:face_rows]
-            face_out[turn, 1, v, :, :] = picked[v][face_rows : 2 * face_rows]
+            other = pltpu.roll(picked[v], SUBLANES // 2, 0)
+            found = jnp.where((index >> 7) < half, picked[v], other)
+            face_out[turn, 0, v, :, :] = found[0:face_rows]
+            face_out[turn, 1, v, :, :] = found[face_rows : 2 * face_rows]
 
     def face_copy(turn, way):
         return pltpu.make_async_remote_copy(
@@ -173,6 +182,14 @@
         )
 
     edge = (g == 0, g == groups - 1)
+
+    def send_faces(turn):
+        for way in range(2):
+            pl.when(jnp.logical_not(edge[1 - way]))(face_copy(turn, way).start)
+
+    def sent_faces(turn):
+        for way in range(2):
+            pl.when(jnp.logical_not(edge[1 - way]))(face_copy(turn, way).wait_send)
 
     def drive_local():
         lane_ids = lax.broadcasted_iota(jnp.int32, (rows, LANES), 1)
@@ -191,7 +208,7 @@
 
     def drive_faces(turn):
         for way in range(2):
-            face_copy(turn, way).wait_recv()
+            pl.when(jnp.logical_not(edge[way]))(face_copy(turn, way).wait_recv)
         tables = []
         for way, coef_ref in ((0, coef_down_ref), (1, coef_up_ref)):
             for j in range(face_rows):
@@ -214,68 +231,84 @@
                     total = total + add
                 drive[v, part, :] = total
 
-    def block_copy(phase, peer, slot):
+    def block_copy(phase, peer, out_slot, in_slot):
         return pltpu.make_async_remote_copy(
-            src_ref=out_buf.at[phase, peer],
-            dst_ref=in_buf.at[phase, slot],
-            send_sem=send_sem.at[phase, peer],
-            recv_sem=recv_sem.at[phase, slot],
+            src_ref=out_buf.at[phase, out_slot],
+            dst_ref=in_buf.at[phase, in_slot],
+            send_sem=send_sem.at[phase, out_slot],
+            recv_sem=recv_sem.at[phase, in_slot],
             device_id={"dom": peer},
             device_id_type=MESH,
         )
 
+    def members(i, sign):
+        found = []
+        for there in (4 + i, 3 - i):
+            for over in RINGS:
+                at = lax.rem(place + SUBLANES + sign * there, SUBLANES)
+                found.append(lax.rem(ring + tall + sign * over, tall) * SUBLANES + at)
+        return found
+
+    def unless_self(i, u, action):
+        if u < SUBLANES - 1:
+            action()
+        else:
+            pl.when(i != tall - 1)(action)
+
     def exchange(phase, load_row, index_ref):
-        def one_ring(i, carry):
-            offset = ring_order(tall - 1 - i)
-            start = pl.multiple_of(lax.rem(ring + offset, tall) * SUBLANES, SUBLANES)
+        def one_group(i, carry):
+            start = pl.multiple_of(i * SUBLANES, SUBLANES)
             picked = pick_block(load_row, index_ref[pl.ds(start, SUBLANES), :])
             for s in range(SUBLANES):
                 for v in range(nvar):
                     out_buf[phase, start + s, v : v + 1, :] = picked[v][s : s + 1]
-            for step in NEAR_FIRST[:0:-1]:
-                block_copy(phase, start + lax.rem(place + step, SUBLANES), d).start()
-
-            @pl.when(offset != 0)
-            def _():
-                block_copy(phase, start + place, d).start()
-
+            for u, peer in enumerate(members(i, 1)):
+                unless_self(i, u, block_copy(phase, peer, start + u, d).start)
             return carry
 
-        lax.fori_loop(0, tall, one_ring, 0)
+        lax.fori_loop(0, tall, one_group, 0)
+
+    def drain(phase):
+        def one_group(i, carry):
+            for u, peer in enumerate(members(i, 1)):
+                unless_self(i, u, block_copy(phase, peer, i * SUBLANES + u, d).wait_send)
+            return carry
+
+        lax.fori_loop(0, tall, one_group, 0)
 
     def merge(phase, load_row, index_ref, out):
         parts = [slice(b * SUBLANES, (b + 1) * SUBLANES) for b in range(blocks)]
+
+        def pool_row(v, r):
+            return in_buf[phase, r, v : v + 1, :]
+
+        def own(b, carry):
+            part = pl.ds(pl.multiple_of(b * SUBLANES, SUBLANES), SUBLANES)
+            picked = pick_block(load_row, index_ref[part, :] - domains * LANES)
+            for v in range(nvar):
+                out[v, part, :] = picked[v]
+            return carry
+
+        lax.fori_loop(0, blocks, own, 0)
+        if phase:
+            drain(phase - 1)
         index = [index_ref[part, :] for part in parts]
         row, lane = [one >> 7 for one in index], [one & 127 for one in index]
-        own_row = [one - domains for one in row]
-
-        def pool_row(v, r):
-            return in_buf[phase, r, v : v + 1, :]
-
-        def own(step, picked):
+
+        def pool(step, picked):
             picked = list(picked)
-            for u in range(SUBLANES):
-                pick_row(picked, load_row, step * SUBLANES + u, own_row, lane, nvar)
+            i = tall - 1 - step
+            peers = members(i, -1)
+            for u, peer in enumerate(peers):
+                unless_self(i, u, block_copy(phase, peer, peer, peer).wait_recv)
+            for b in range(blocks):
+                mine = picked[b * nvar : (b + 1) * nvar]
+                for peer in peers:
+                    pick_row(mine, pool_row, peer, row[b : b + 1], lane[b : b + 1], nvar)
+                picked[b * nvar : (b + 1) * nvar] = mine
             return tuple(picked)
 
-        def pool(i, picked):
-            picked = list(picked)
-            offset = ring_order(i)
-            start = lax.rem(ring + offset, tall) * SUBLANES
-            for step in NEAR_FIRST:
-                r = start + lax.rem(place + step, SUBLANES)
-                if step:
-                    block_copy(phase, r, r).wait_recv()
-                else:
-
-                    @pl.when(offset != 0)
-                    def _():
-                        block_copy(phase, r, r).wait_recv()
-
-                pick_row(picked, pool_row, r, row, lane, nvar)
-            return tuple(picked)
-
-        picked = lax.fori_loop(0, blocks, own, tuple([zero] * (nvar * blocks)))
+        picked = tuple(out[v, part, :] for part in parts for v in range(nvar))
         picked = lax.fori_loop(0, tall, pool, picked)
         for b, part in enumerate(parts):
             for v in range(nvar):
@@ -319,8 +352,15 @@
         lax.fori_loop(0, length // UNROLL, forward, ends)
         lax.fori_loop(0, length // UNROLL, backward, ends)
 
+    def order_maps(i, carry):
+        for u, peer in enumerate(members(i, 1)):
+            for ref, ordered in ((send_idx_ref, send_map), (ret_idx_ref, ret_map)):
+                ordered[pl.ds(i * SUBLANES + u, 1), :] = ref[pl.ds(peer, 1), :]
+        return carry
+
     pick_faces(0)
     drive_local()
+    lax.fori_loop(0, tall, order_maps, 0)
     for which, ref in ((0, face_down_ref), (1, face_up_ref)):
         cells = ref[0, 0:1, :]
         number = (lax.broadcasted_iota(jnp.int32, (1, faces), 1) + 1).astype(jnp.float32)
@@ -336,41 +376,33 @@
         inv[which] = found.astype(jnp.int32)
 
     pl.semaphore_wait(barrier, domains + 1)
-    for way in range(2):
-        face_copy(0, way).start()
+    send_faces(0)
 
     for sweep in range(SWEEPS):
         if sweep:
             drive_local()
         drive_faces(sweep)
-        exchange(2 * sweep, drive_row, send_idx_ref)
+        exchange(2 * sweep, drive_row, send_map)
         merge(2 * sweep, drive_row, line_idx_ref, lines)
         if sweep == 0:
             for i in late:
                 fetches[i].wait()
         solve()
-        exchange(2 * sweep + 1, lines_row, ret_idx_ref)
+        exchange(2 * sweep + 1, lines_row, ret_map)
         merge(2 * sweep + 1, lines_row, cell_idx_ref, state)
         pick_faces(sweep + 1)
-        for way in range(2):
-            face_copy(sweep + 1, way).start()
-    sol_copy = pltpu.make_async_copy(state, sol_hbm, result_sem.at[0])
+        send_faces(sweep + 1)
+    sol_copy = pltpu.make_async_copy(state, sol_out, result_sem.at[0])
     sol_copy.start()
     drive_local()
+    drain(2 * SWEEPS - 1)
+    for turn in range(SWEEPS):
+        sent_faces(turn)
     drive_faces(SWEEPS)
-    drv_copy = pltpu.make_async_copy(drive, drv_hbm, result_sem.at[1])
+    drv_copy = pltpu.make_async_copy(drive, drv_out, result_sem.at[1])
     drv_copy.start()
 
-    for turn in range(SWEEPS + 1):
-        for way in range(2):
-            face_copy(turn, way).wait_send()
-
-    def drain(i, carry):
-        for phase in range(2 * SWEEPS):
-            block_copy(phase, lax.rem(d + i, domains), d).wait_send()
-        return carry
-
-    lax.fori_loop(1, domains, drain, 0)
+    sent_faces(SWEEPS)
     sol_copy.wait()
     drv_copy.wait()
 
@@ -396,7 +428,7 @@
     pool = pltpu.VMEM((2 * SWEEPS, domains, nvar, LANES), f32)
     turns = SWEEPS + 1
     faces = pltpu.VMEM((turns, 2, nvar, face_rows, LANES), f32)
-    out = jax.ShapeDtypeStruct(field, f32)
+    out = pltpu.VMEM(field, f32)
     sol, drv = pl.pallas_call(
         functools.partial(kernel, nvar, groups, domains),
         out_shape=(out, out),
@@ -409,6 +441,8 @@
             grid_field,
             pool,
             pool,
+            pltpu.VMEM(send_cell.shape, jnp.int32),
+            pltpu.VMEM(send_cell.shape, jnp.int32),
             pltpu.VMEM((SUBLANES, LANES), jnp.int32),
             pltpu.VMEM((2, rows, LANES), jnp.int32),
             faces,

time: 62.4 us -> 51 us (0.82)
  Pallas kernels: 59.9 us -> 49.5 us
  local copies, waits for them, and re-layouts: 1.73 us -> 0.8 us
    pallas_call x1, Pallas kernels: 59.9 us -> 49.5 us  [shards(): pl.pallas_call(functools.partial(kernel, nvar, groups, domains), out_shap...]
    reshape x1, local copies, waits for them, and re-layouts: 1.73 us -> 0.8 us  [shards(): return (sol.reshape(nvar, cell_count), drv.reshape(nvar, cell_count))]
where the time goes in v3:
time: 51 us; the launch traced here: 50.9 us
  Pallas kernels  49.5 us (97%)
  local copies, waits for them, and re-layouts  0.8 us (2%)
  between operations  0.64 us (1%)
    pallas_call x1, Pallas kernels, shards(): pl.pallas_call(functools.partial(kernel, nvar, groups, domains), out_shap...  49.5 us

profile of v3, /device:TPU:1, one launch (start us, length us, event | category | flops | bytes accessed | tf_op | source)
XLA Modules:
  0.0 50.9 jit_solution(5393803705243576068)
XLA Ops:
  0.6 49.5 %relax.1 = (f32[5,32,128]{2,1,0:T(8,128)S(1)}, f32[5,32,128]{2,1,0:T(8,128)S(1)}) custom-call(f32[5,4096]{1,0:T(8,128)} %flow_hbm.1, f32[5,4096]{1,0:T(8,128)} %rhs_hbm.1, f32[32,128]{1,0:T(8,128)} %bitcast.16, f32[25,32,128]{2,1,0:T(8,128)} %bitcast.13, f32[25,32,128]{2,1,0:T(8,128)} %bitcast.14, f32[25,32,128]{2,1,0:T(8,128)} %bitcast.15, ...), custom_call_target="tpu_custom_call" | custom-call | tf_op jit(solution)/shard_map/relax/pallas_call | solution.py:432
  50.1 0.8 %copy_bitcast_fusion = (f32[5,4096]{1,0:T(8,128)}, f32[5,4096]{1,0:T(8,128)}) fusion(f32[1,5,32,128]{3,2,1,0:T(8,128)S(1)} %bitcast.12, f32[1,5,32,128]{3,2,1,0:T(8,128)S(1)} %bitcast.11), kind=kLoop, calls=%fused_computation | loop fusion | bytes 327680 | tf_op jit(solution)/shard_map/reshape | solution.py:460
